TPU v7x, 128 devices: a whole 4x4x4 slice. The times are simulated.
128 devices in a mesh: req: 32 (over z, x, core), tp: 4 (over y).
Axes of the slice: x: 4, y: 4, z: 4, core: 2. Of those that a mesh axis runs over, the one named last changes fastest.
Arguments:
- tokens: bfloat16 [16384, 2560], P('req'), may hold values from -6 to 6
- lengths: int32 [32], P('req'), may hold values from 1 to 512, as said below
- page_slot: int32 [128], replicated, may hold values from 0 to 127, as said below
- trainer_layout: int32 [128], replicated, may hold values from 0 to 127, each once
- trainer_qkv: float32 [2560, 3840], P(('req', 'tp'))
- trainer_gateup: float32 [2560, 13824], P(('req', 'tp')), may hold values from -0.125 to 0.125
- attn_gain: float32 [2560], replicated, may hold values from 0.1 to 1.9
- ffn_gain: float32 [2560], replicated, may hold values from 0.1 to 1.9
- out_proj: bfloat16 [2560, 2560], P('tp'), may hold values from -0.125 to 0.125
- down_proj: bfloat16 [6912, 2560], P('tp'), may hold values from -0.078125 to 0.078125
Outputs:
- layer_out: bfloat16 [16384, 2560], P(('req', 'tp'))
- kv_cache: bfloat16 [128, 128, 1280], P('req', None, 'tp')
Inputs may be any that keep to these rules, and one draw needn't show every extreme that they name: `lengths`: heavy-tailed; some request has exactly 512. `page_slot`: a permutation; pool slot s belongs to request device s // 4; the 4 pages of one request belong to 4 different devices. `trainer_layout`: a permutation; shard s is the trainer shard on the device with index s over req and tp together.
All inputs are finite; a program needn't handle non-finite values.
Results may differ from a plain program's by a relative error of at most 0.0065.
The roundings to bfloat16 on the way count: a program that leaves them out, or rounds other values in their place, can miss the bound.
Values may be sent and summed in bfloat16 or wider, within the bound.
A program may use at most 192 MiB of HBM per device.

v0:
```python
import jax
import jax.numpy as jnp
from jax import lax
from jax.sharding import PartitionSpec as P

HD = 80
PAGE = 128
eps_norm = 1e-05
theta_base = 10000.0


def normed(values, gain):
    scale = lax.rsqrt(jnp.mean(values * values, axis=-1, keepdims=True) + eps_norm)
    return (values * scale * gain).astype(jnp.bfloat16)


def rotary(field, head_dim):
    half = head_dim // 2
    count = field.shape[0]
    freq = theta_base ** (-jnp.arange(half, dtype=jnp.float32) * 2.0 / head_dim)
    angles = jnp.arange(count, dtype=jnp.float32)[:, None] * freq[None, :]
    cosine = jnp.cos(angles)[:, None, :]
    sine = jnp.sin(angles)[:, None, :]
    first = field[..., :half]
    second = field[..., half:]
    return jnp.concatenate(
        [first * cosine - second * sine, second * cosine + first * sine], axis=-1
    )


def body(
    tokens,
    lengths,
    page_slot,
    trainer_layout,
    trainer_qkv,
    trainer_gateup,
    attn_gain,
    ffn_gain,
    out_proj,
    down_proj,
):
    n_tp = lax.axis_size("tp")
    n_req = lax.axis_size("req")
    devices = n_tp * n_req
    rows_each = trainer_qkv.shape[0]
    seq_len = tokens.shape[0]
    model_dim = tokens.shape[1]
    head_dim = HD
    local_heads = out_proj.shape[0] // head_dim
    group_cols = trainer_qkv.shape[1] // n_tp
    local_kv = (group_cols // head_dim - local_heads) // 2
    group = local_heads // local_kv
    q_cols = local_heads * head_dim
    k_cols = local_kv * head_dim
    ff_local = down_proj.shape[0]
    qkv_half, gu_half = (
        lax.all_to_all(
            trainer_qkv.astype(jnp.bfloat16), "tp", split_axis=1, concat_axis=0, tiled=True
        ),
        lax.all_to_all(
            trainer_gateup.astype(jnp.bfloat16), "tp", split_axis=1, concat_axis=0, tiled=True
        ),
    )
    x_f = tokens.astype(jnp.float32)
    x_norm = normed(x_f, attn_gain)
    inverse = (
        jnp.zeros((devices,), jnp.int32)
        .at[trainer_layout]
        .set(jnp.arange(devices, dtype=jnp.int32))
    )
    qkv_all, gu_all = (
        lax.all_gather(qkv_half, "req", axis=0, tiled=True),
        lax.all_gather(gu_half, "req", axis=0, tiled=True),
    )
    qkv_weight = qkv_all.reshape(devices, rows_each, qkv_all.shape[1])[inverse].reshape(
        model_dim, qkv_all.shape[1]
    )
    gu_weight = gu_all.reshape(devices, rows_each, gu_all.shape[1])[inverse].reshape(
        model_dim, gu_all.shape[1]
    )
    joined = jnp.dot(x_norm, qkv_weight, preferred_element_type=jnp.float32)
    query = rotary(joined[:, :q_cols].reshape(seq_len, local_heads, head_dim), head_dim)
    keys = rotary(
        joined[:, q_cols : q_cols + k_cols].reshape(seq_len, local_kv, head_dim), head_dim
    )
    query16 = query.astype(jnp.bfloat16).reshape(seq_len, local_kv, group, head_dim)
    keys16 = keys.astype(jnp.bfloat16)
    values16 = (
        joined[:, q_cols + k_cols :].reshape(seq_len, local_kv, head_dim).astype(jnp.bfloat16)
    )
    scores = jnp.einsum(
        "qkgd,skd->kgqs", query16, keys16, preferred_element_type=jnp.float32
    ) * head_dim ** (-0.5)
    slots = jnp.arange(seq_len, dtype=jnp.int32)
    length = lengths[0]
    allowed = (slots[None, :] <= slots[:, None]) & (slots[None, :] < length)
    scores = jnp.where(allowed[None, None], scores, -1e30)
    probs = jax.nn.softmax(scores, axis=-1).astype(jnp.bfloat16)
    context = jnp.einsum(
        "kgqs,skd->qkgd", probs, values16, preferred_element_type=jnp.float32
    ).astype(jnp.bfloat16)
    partial_out = jnp.dot(
        context.reshape(seq_len, q_cols), out_proj, preferred_element_type=jnp.float32
    )
    share = seq_len // n_tp
    tp_index = lax.axis_index("tp")
    mixed = lax.psum(partial_out, "tp")
    resid = x_f + mixed
    h_norm = normed(resid, ffn_gain)
    resid_share = lax.dynamic_slice_in_dim(resid, tp_index * share, share, 0)
    projected = jnp.dot(h_norm, gu_weight, preferred_element_type=jnp.float32)
    hidden = (jax.nn.silu(projected[:, :ff_local]) * projected[:, ff_local:]).astype(jnp.bfloat16)
    down = jnp.dot(hidden, down_proj, preferred_element_type=jnp.float32)
    added = lax.psum_scatter(down, "tp", scatter_dimension=0, tiled=True)
    share_slots = tp_index * share + jnp.arange(share, dtype=jnp.int32)
    live_share = (share_slots < length).astype(jnp.float32)
    layer_out = ((resid_share + added) * live_share[:, None]).astype(jnp.bfloat16)
    live_rows = (slots < length)[:, None]
    key_rows = keys16.reshape(seq_len, k_cols)
    value_rows = values16.reshape(seq_len, k_cols)
    cache_rows = jnp.concatenate(
        [
            jnp.where(live_rows, key_rows, jnp.zeros_like(key_rows)),
            jnp.where(live_rows, value_rows, jnp.zeros_like(value_rows)),
        ],
        axis=1,
    )
    pages = cache_rows.reshape(seq_len // PAGE, PAGE, 2 * k_cols)
    pool_size = pages.shape[0]
    owner = lax.axis_index("req")
    targets = owner * pool_size + jnp.arange(pool_size, dtype=jnp.int32)
    picks = (page_slot[:, None] == targets[None, :]).astype(jnp.bfloat16)
    pool = jnp.einsum(
        "np,nsc->psc",
        picks,
        lax.all_gather(pages, "req", axis=0, tiled=True),
        preferred_element_type=jnp.float32,
    )
    kv_cache = pool.astype(jnp.bfloat16)
    return (layer_out, kv_cache)


def solution(mesh):
    return jax.shard_map(
        body,
        mesh=mesh,
        in_specs=(
            P("req", None),
            P("req"),
            P(),
            P(),
            P(("req", "tp"), None),
            P(("req", "tp"), None),
            P(),
            P(),
            P("tp", None),
            P("tp", None),
        ),
        out_specs=(P(("req", "tp"), None), P("req", None, "tp")),
        check_vma=False,
    )
```

profile of v0, /device:TPU:1, one launch (start us, length us, event | category | flops | bytes accessed | tf_op | source)
XLA Modules:
  0.0 472.2 jit_solution(814724774709201183)
XLA Ops:
  7.2 1.2 convert_element_type.60
  8.4 0.9 all_to_all.28
  9.3 1.0 copy.18
  10.3 10.0 %all_to_all.38 = bf16[20,4,960]{2,0,1:T(8,128)(2,1)S(1)} all-to-all(bf16[20,4,960]{2,0,1:T(8,128)(2,1)S(1)} %copy.18), channel_id=1, replica_groups=mesh['req'=32,'tp'=4] {'tp'}, dimensions={1} | all-to-all | bytes 307200 | tf_op jit(solution)/shard_map/all_to_all | solution.py:58
  22.4 1.0 scatter_custom_fusion
  23.4 2.3 fusion.4
  26.1 0.8 fusion.26
  27.0 43.9 %all-gather.4.cloned.1.call-done = bf16[2560,960]{1,0:T(8,128)(2,1)} async-done(((bf16[80,960]{1,0:T(8,128)(2,1)}), bf16[2560,960]{1,0:T(8,128)(2,1)}) %all-gather.4.cloned.1.call-update) | async-done | bytes 4915216 | tf_op jit(solution)/shard_map/all_gather | solution.py:73
  70.9 9.7 %reshape.159 = bf16[128,20,960]{2,1,0:T(8,128)(2,1)} reshape(bf16[2560,960]{1,0:T(8,128)(2,1)} %all-gather.4.cloned.1.call-done) | data formatting | bytes 9830400 | tf_op jit(solution)/shard_map/reshape | solution.py:76
  80.6 6.4 %gather_fusion = bf16[128,20,960]{2,1,0:T(8,128)(2,1)} fusion(bf16[128,20,960]{2,1,0:T(8,128)(2,1)} %reshape.159, s32[1024]{0:T(1024)S(1)} %pad_clamp_fusion), kind=kCustom, calls=%fused_computation | custom fusion | bytes 9830912 | tf_op jit(solution)/shard_map/gather | solution.py:76
  87.0 9.8 %reshape.160 = bf16[2560,960]{1,0:T(8,128)(2,1)} reshape(bf16[128,20,960]{2,1,0:T(8,128)(2,1)} %gather_fusion) | data formatting | bytes 9830400 | tf_op jit(solution)/shard_map/reshape | solution.py:76
  96.8 6.2 %fusion.13 = f32[512,960]{0,1:T(8,128)S(1)} fusion(bf16[2560,960]{1,0:T(8,128)(2,1)} %reshape.160, bf16[512,2560]{1,0:T(8,128)(2,1)} %param.10, f32[2560]{0:T(1024)S(1)} %copy-done.7, f32[512]{0:T(512)S(1)} %add_rsqrt_fusion.1), kind=kOutput, calls=%fused_computation.25 | convolution fusion | flops 2521825280 | bytes 9515008 | tf_op jit(solution)/shard_map/dot_general | solution.py:82
  103.9 1.0 subtract_convert_fusion
  105.6 7.6 %fusion.49 = (f32[2,4,512]{2,1,0:T(4,128)S(1)}, f32[2,4,512,512]{2,3,1,0:T(8,128)}) fusion(pred[512,512]{0,1:T(8,128)(4,1)} %fusion.26, bf16[512,2,4,40]{0,3,2,1:T(8,128)(2,1)} %bitcast.65, bf16[512,2,4,40]{0,3,2,1:T(8,128)(2,1)} %bitcast.64, bf16[512,2,40]{0,2,1:T(8,128)(2,1)} %get-tuple-element.15, bf16[512,2,40]{0,2,1:T(8,128)(2,1)S(1)} %get-tuple-element.14), kind=kOutput, calls=%fused_computation.76 | convolution fusion | flops 345571840 | bytes 9486336 | tf_op jit(solution)/shard_map/sub | solution.py:99
  113.2 4.2 fusion.22
  117.4 4.6 fusion.54
  122.1 2.4 convert_element_type.68
  124.5 1.3 all_to_all.32
  125.9 21.6 %all_to_all.39 = bf16[20,4,3456]{2,0,1:T(8,128)(2,1)} all-to-all(bf16[20,4,3456]{2,0,1:T(8,128)(2,1)S(1)} %copy.20), channel_id=1, replica_groups=mesh['req'=32,'tp'=4] {'tp'}, dimensions={1} | all-to-all | bytes 1105920 | tf_op jit(solution)/shard_map/all_to_all | solution.py:61
  147.5 2.0 all_to_all.35
  150.8 86.5 %all-reduce.2.cloned.1.call-done = f32[512,2560]{1,0:T(8,128)} async-done(((f32[512,2560]{1,0:T(8,128)}), f32[512,2560]{1,0:T(8,128)}) %all-reduce.2.cloned.1.call-update) | async-done | bytes 5242896 | tf_op jit(solution)/shard_map/psum | solution.py:108
  237.4 5.4 %multiply_reduce_fusion = (f32[512]{0:T(512)S(1)}, f32[512,2560]{1,0:T(8,128)}) fusion(f32[512,2560]{1,0:T(8,128)} %all-reduce.2.cloned.1.call-done, bf16[512,2560]{1,0:T(8,128)(2,1)S(1)} %copy-done.2), kind=kLoop, calls=%fused_computation.17 | loop fusion | flops 5242368 | bytes 13109248 | tf_op jit(solution)/shard_map/reduce_sum | solution.py:13
  242.8 72.6 %all-gather.6.cloned.1.call-done = bf16[2560,3456]{1,0:T(8,128)(2,1)} async-done(((bf16[80,3456]{1,0:T(8,128)(2,1)}), bf16[2560,3456]{1,0:T(8,128)(2,1)}) %all-gather.6.cloned.1.call-update) | async-done | bytes 17694736 | tf_op jit(solution)/shard_map/all_gather | solution.py:74
  315.4 24.5 %reshape.164 = bf16[128,20,3456]{2,1,0:T(8,128)(2,1)} reshape(bf16[2560,3456]{1,0:T(8,128)(2,1)} %all-gather.6.cloned.1.call-done) | data formatting | bytes 35389440 | tf_op jit(solution)/shard_map/reshape | solution.py:79
  339.9 17.0 %gather_fusion.1 = bf16[128,20,3456]{2,1,0:T(8,128)(2,1)} fusion(bf16[128,20,3456]{2,1,0:T(8,128)(2,1)} %reshape.164, s32[1024]{0:T(1024)S(1)} %pad_clamp_fusion), kind=kCustom, calls=%fused_computation.1 | custom fusion | bytes 35389952 | tf_op jit(solution)/shard_map/gather | solution.py:79
  356.9 25.1 %reshape.165 = bf16[2560,3456]{1,0:T(8,128)(2,1)} reshape(bf16[128,20,3456]{2,1,0:T(8,128)(2,1)} %gather_fusion.1) | data formatting | bytes 35389440 | tf_op jit(solution)/shard_map/reshape | solution.py:79
  382.0 15.3 %fusion.12 = f32[512,3456]{1,0:T(8,128)S(1)} fusion(bf16[2560,3456]{1,0:T(8,128)(2,1)} %reshape.165, f32[512,2560]{1,0:T(8,128)} %get-tuple-element.11, f32[2560]{0:T(1024)S(1)} %copy-done.8, f32[512]{0:T(512)S(1)} %add_rsqrt_fusion), kind=kOutput, calls=%fused_computation.24 | convolution fusion | flops 9063628800 | bytes 30027776 | tf_op jit(solution)/shard_map/dot_general | solution.py:112
  397.3 10.4 %fusion.19 = f32[512,2560]{1,0:T(8,128)} fusion(bf16[1728,2560]{1,0:T(8,128)(2,1)} %param.19, f32[512,3456]{1,0:T(8,128)S(1)} %fusion.12), kind=kOutput, calls=%fused_computation.30 | convolution fusion | flops 4535156736 | bytes 21430272 | tf_op jit(solution)/shard_map/dot_general | solution.py:114
  408.4 9.9 %fusion.23 = bf16[4,128,320]{1,0,2:T(4,128)(2,1)S(1)} fusion(bf16[128,128,320]{1,2,0:T(8,128)(2,1)} %all-gather.8.cloned.1.call-done, s32[128]{0:T(128)S(1)} %copy-done.6, s32[4]{0:T(128)S(1)} %iota_add_fusion), kind=kOutput, calls=%fused_computation.34 | convolution fusion | flops 42107392 | bytes 10813968 | tf_op jit(solution)/shard_map/np,nsc->psc/dot_general | solution.py:134
  418.3 0.8 copy.24
  419.1 43.9 %reduce-scatter.2.cloned.1.call-done = f32[128,2560]{1,0:T(8,128)} async-done(((f32[512,2560]{1,0:T(8,128)}), f32[128,2560]{1,0:T(8,128)}) %reduce-scatter.2.cloned.1.call-update) | async-done | bytes 1310736 | tf_op jit(solution)/shard_map/reduce_scatter | solution.py:115
  462.9 2.7 multiply_convert_fusion.2
  (52 shorter events, 5.4 us)
Async XLA Ops:
  7.2 110.3 %copy-start = (bf16[640,2560]{1,0:T(8,128)(2,1)S(1)}, bf16[640,2560]{1,0:T(8,128)(2,1)}, u32[]{:S(2)}) copy-start(bf16[640,2560]{1,0:T(8,128)(2,1)} %param.18) | copy-start | bytes 9830404
  7.2 63.7 %all-gather.4.cloned.1.call-start = ((), (), s32[]{:S(2)}) async-start(), calls=%async_computation.3 | async-start | bytes 5406720 | tf_op jit(solution)/shard_map/all_gather | solution.py:73
  21.0 216.3 %all-reduce.2.cloned.1.call-start = ((), (), s32[]{:S(2)}) async-start(), calls=%async_computation.4 | async-start | bytes 10485760 | tf_op jit(solution)/shard_map/psum | solution.py:108
  87.0 9.8 %copy-start.7 = (f32[2560]{0:T(1024)S(1)}, f32[2560]{0:T(1024)}, u32[]{:S(2)}) copy-start(f32[2560]{0:T(1024)} %param.16) | copy-start | bytes 30724
  105.6 7.6 %copy-start.5 = (bf16[512,160]{0,1:T(8,128)(2,1)S(1)}, bf16[512,160]{0,1:T(8,128)(2,1)}, u32[]{:S(2)}) copy-start(bf16[512,160]{0,1:T(8,128)(2,1)} %get-tuple-element.9) | copy-start | bytes 491524
  122.0 27.8 %copy-start.3 = (bf16[20,4,8,128]{3,2,1,0:T(8,128)(2,1)S(1)}, bf16[20,4,8,128]{3,2,1,0:T(8,128)(2,1)}, u32[]{:S(2)}) copy-start(bf16[20,4,8,128]{3,2,1,0:T(8,128)(2,1)} %get-tuple-element.8) | copy-start | bytes 491524
  122.0 27.8 %copy-start.4 = (bf16[512,2,40]{0,2,1:T(8,128)(2,1)S(1)}, bf16[512,2,40]{0,2,1:T(8,128)(2,1)}, u32[]{:S(2)}) copy-start(bf16[512,2,40]{0,2,1:T(8,128)(2,1)} %get-tuple-element.15) | copy-start | bytes 245764
  122.0 115.3 %copy-start.2 = (bf16[512,2560]{1,0:T(8,128)(2,1)S(1)}, bf16[512,2560]{1,0:T(8,128)(2,1)}, u32[]{:S(2)}) copy-start(bf16[512,2560]{1,0:T(8,128)(2,1)} %param.10) | copy-start | bytes 7864324
  122.1 193.3 %all-gather.6.cloned.1.call-start = ((), (), s32[]{:S(2)}) async-start(), calls=%async_computation.5 | async-start | bytes 18247680 | tf_op jit(solution)/shard_map/all_gather | solution.py:74
  149.6 258.2 %all-gather.8.cloned.1.call-start = ((), (), s32[]{:S(2)}) async-start(), calls=%async_computation.7 | async-start | bytes 10813440 | tf_op jit(solution)/shard_map/all_gather | solution.py:137
  150.8 312.2 %reduce-scatter.2.cloned.1.call-start = ((), (), s32[]{:S(2)}) async-start(), calls=%async_computation.6 | async-start | bytes 6553600 | tf_op jit(solution)/shard_map/reduce_scatter | solution.py:115
  356.9 25.1 %copy-start.8 = (f32[2560]{0:T(1024)S(1)}, f32[2560]{0:T(1024)}, u32[]{:S(2)}) copy-start(f32[2560]{0:T(1024)} %param.17) | copy-start | bytes 30724
  407.7 0.7 copy-start.6
  407.8 57.9 %copy-start.1 = (bf16[640,2560]{1,0:T(8,128)(2,1)S(1)}, bf16[640,2560]{1,0:T(8,128)(2,1)}, u32[]{:S(2)}) copy-start(bf16[640,2560]{1,0:T(8,128)(2,1)} %param.18) | copy-start | bytes 9830404
Sparse Core Ops, SparseCore 0:
  21.1 49.7 all-gather.3
  122.2 115.1 all-reduce.1
  240.3 75.0 all-gather.5
  318.1 57.3 all-gather.7
  407.9 55.0 reduce-scatter.1
where the time goes:
time: 474 us; the launch traced here: 472 us
  waiting for transfers between devices  247 us (52%)
  local copies, waits for them, and re-layouts  101 us (21%)
  matrix products  58.2 us (12%)
  blocking collectives  31.6 us (7%)
  other arithmetic  19.2 us (4%)
  between operations  14.6 us (3%)
    psum x1, waiting for transfers between devices, body(): mixed = lax.psum(partial_out, 'tp')  86.5 us
    all_gather x1, waiting for transfers between devices, body(): lax.all_gather(gu_half, 'req', axis=0, tiled=True)  72.6 us
    reshape x2, local copies, waits for them, and re-layouts, body(): gu_all.reshape(devices, rows_each, gu_all.shape[1])[inverse]  49.7 us
    all_gather x1, waiting for transfers between devices, body(): lax.all_gather(qkv_half, 'req', axis=0, tiled=True)  43.9 us
    reduce_scatter x1, waiting for transfers between devices, body(): added = lax.psum_scatter(down, 'tp', scatter_dimension=0, tiled=True)  43.9 us
    all_to_all x1, blocking collectives, body(): lax.all_to_all(trainer_gateup.astype(jnp.bfloat16), 'tp', split_axis=1, c...  21.6 us
    reshape x2, local copies, waits for them, and re-layouts, body(): qkv_all.reshape(devices, rows_each, qkv_all.shape[1])[inverse]  19.5 us
    gather x1, local copies, waits for them, and re-layouts, body(): gu_all.reshape(devices, rows_each, gu_all.shape[1])[inverse]  17 us
  transfers between devices with their start and end apart: 5, of which 4 were waited for; matrix products, arithmetic and copies ran while one was open for 25% of the time, Pallas kernels for 0%

commit v1 on v0

--- a/solution.py
+++ b/solution.py
@@ -70,7 +70,9 @@
         .set(jnp.arange(devices, dtype=jnp.int32))
     )
     qkv_all, gu_all = (
-        lax.all_gather(qkv_half, "req", axis=0, tiled=True),
+        jnp.concatenate(
+            lax.all_to_all(jnp.stack([qkv_half] * lax.axis_size("req")), "req", 0, 0), axis=0
+        ),
         lax.all_gather(gu_half, "req", axis=0, tiled=True),
     )
     qkv_weight = qkv_all.reshape(devices, rows_each, qkv_all.shape[1])[inverse].reshape(

time: 474 us -> 431 us (0.909)
  waiting for transfers between devices: 247 us -> 190 us
  starting transfers between devices: 0.39 us -> 10.6 us
  local copies, waits for them, and re-layouts: 101 us -> 106 us
    all_gather x1, waiting for transfers between devices: 72.6 us -> 0.01 us  [body(): lax.all_gather(gu_half, 'req', axis=0, tiled=True)]
    all_to_all x0 -> x1, waiting for transfers between devices: none -> 56.2 us  [body(): lax.all_to_all(jnp.stack([qkv_half] * lax.axis_size('req')), 'req', 0, 0)]
    all_gather x1 -> x0, waiting for transfers between devices: 43.9 us -> none  [body(): lax.all_gather(qkv_half, 'req', axis=0, tiled=True)]
    another operation x0 -> x3, local copies, waits for them, and re-layouts: none -> 14.3 us  [the longest x1 9.72 us: body(): qkv_all.reshape(devices, rows_each, qkv_all.shape[1])[inverse]]
    all_to_all x0 -> x1, starting transfers between devices: none -> 10.2 us  [body(): lax.all_to_all(jnp.stack([qkv_half] * lax.axis_size('req')), 'req', 0, 0)]
    reshape x2 -> x1, local copies, waits for them, and re-layouts: 19.5 us -> 9.8 us  [body(): qkv_all.reshape(devices, rows_each, qkv_all.shape[1])[inverse]]
  transfers between devices with their start and end apart: 5 -> 5, of which waited for: 4 -> 3; matrix products, arithmetic and copies ran while one was open for 25% -> 27% of each run, Pallas kernels for 0% -> 0%
where the time goes in v1:
time: 431 us; the launch traced here: 428 us
  waiting for transfers between devices  190 us (44%)
  local copies, waits for them, and re-layouts  106 us (25%)
  matrix products  58.1 us (13%)
  blocking collectives  29.2 us (7%)
  other arithmetic  18.5 us (4%)
  between operations  16.4 us (4%)
  starting transfers between devices  10.6 us (2%)
    psum x1, waiting for transfers between devices, body(): mixed = lax.psum(partial_out, 'tp')  89.1 us
    all_to_all x1, waiting for transfers between devices, body(): lax.all_to_all(jnp.stack([qkv_half] * lax.axis_size('req')), 'req', 0, 0)  56.2 us
    reshape x2, local copies, waits for them, and re-layouts, body(): gu_all.reshape(devices, rows_each, gu_all.shape[1])[inverse]  49.7 us
    reduce_scatter x1, waiting for transfers between devices, body(): added = lax.psum_scatter(down, 'tp', scatter_dimension=0, tiled=True)  44.2 us
    all_to_all x1, blocking collectives, body(): lax.all_to_all(trainer_gateup.astype(jnp.bfloat16), 'tp', split_axis=1, c...  19.2 us
    gather x1, local copies, waits for them, and re-layouts, body(): gu_all.reshape(devices, rows_each, gu_all.shape[1])[inverse]  17.7 us
    dot_general x1, matrix products, body(): projected = jnp.dot(h_norm, gu_weight, preferred_element_type=jnp.float32)  15.3 us
    dot_general x1, matrix products, body(): down = jnp.dot(hidden, down_proj, preferred_element_type=jnp.float32)  10.4 us
  transfers between devices with their start and end apart: 5, of which 3 were waited for; matrix products, arithmetic and copies ran while one was open for 27% of the time, Pallas kernels for 0%

profile of v1, /device:TPU:1, one launch (start us, length us, event | category | flops | bytes accessed | tf_op | source)
XLA Modules:
  0.0 428.2 jit_solution(16896642384340402879)
XLA Ops:
  8.0 1.2 convert_element_type.60
  9.2 0.9 all_to_all.29
  10.1 1.0 copy.18
  11.1 10.0 %all_to_all.40 = bf16[20,4,960]{2,0,1:T(8,128)(2,1)S(1)} all-to-all(bf16[20,4,960]{2,0,1:T(8,128)(2,1)S(1)} %copy.18), channel_id=1, replica_groups=mesh['req'=32,'tp'=4] {'tp'}, dimensions={1} | all-to-all | bytes 307200 | tf_op jit(solution)/shard_map/all_to_all | solution.py:58
  21.8 3.9 stack.5
  25.7 10.2 %all-to-all-start.1 = ((bf16[32,80,960]{2,1,0:T(8,128)(2,1)}), bf16[32,80,960]{2,1,0:T(8,128)(2,1)}, u32[]{:S(2)}, u32[]{:S(2)}) async-start(bf16[32,80,960]{2,1,0:T(8,128)(2,1)} %stack.5), calls=%async_computation.1 | async-start | bytes 10485760 | tf_op jit(solution)/shard_map/all_to_all | solution.py:74
  36.6 1.0 scatter_custom_fusion
  37.6 2.3 fusion.4
  40.4 0.8 fusion.26
  41.2 56.2 %all-to-all-done.1 = bf16[32,80,960]{2,1,0:T(8,128)(2,1)} async-done(((bf16[32,80,960]{2,1,0:T(8,128)(2,1)}), bf16[32,80,960]{2,1,0:T(8,128)(2,1)}, u32[]{:S(2)}, u32[]{:S(2)}) %all-to-all-start.1) | async-done | bytes 4915232 | tf_op jit(solution)/shard_map/all_to_all | solution.py:74
  97.4 9.7 %reshape_reshape.3 = bf16[128,20,960]{2,1,0:T(8,128)(2,1)} reshape(bf16[32,80,960]{2,1,0:T(8,128)(2,1)} %all-to-all-done.1) | data formatting | bytes 9830400 | tf_op jit(solution)/shard_map/reshape;reshape | solution.py:78
  107.1 6.4 %gather_fusion = bf16[128,20,960]{2,1,0:T(8,128)(2,1)} fusion(bf16[128,20,960]{2,1,0:T(8,128)(2,1)} %reshape_reshape.3, s32[1024]{0:T(1024)S(1)} %pad_clamp_fusion), kind=kCustom, calls=%fused_computation | custom fusion | bytes 9830912 | tf_op jit(solution)/shard_map/gather | solution.py:78
  113.5 9.8 %reshape.159 = bf16[2560,960]{1,0:T(8,128)(2,1)} reshape(bf16[128,20,960]{2,1,0:T(8,128)(2,1)} %gather_fusion) | data formatting | bytes 9830400 | tf_op jit(solution)/shard_map/reshape | solution.py:78
  123.3 6.2 %fusion.13 = f32[512,960]{0,1:T(8,128)S(1)} fusion(bf16[2560,960]{1,0:T(8,128)(2,1)} %reshape.159, bf16[512,2560]{1,0:T(8,128)(2,1)} %param.10, f32[2560]{0:T(1024)S(1)} %copy-done.7, f32[512]{0:T(512)S(1)} %add_rsqrt_fusion.1), kind=kOutput, calls=%fused_computation.25 | convolution fusion | flops 2521825280 | bytes 9515008 | tf_op jit(solution)/shard_map/dot_general | solution.py:84
  130.3 1.0 subtract_convert_fusion
  132.1 7.6 %fusion.49 = (f32[2,4,512]{2,1,0:T(4,128)S(1)}, f32[2,4,512,512]{2,3,1,0:T(8,128)}) fusion(pred[512,512]{0,1:T(8,128)(4,1)} %fusion.26, bf16[512,2,4,40]{0,3,2,1:T(8,128)(2,1)} %bitcast.65, bf16[512,2,4,40]{0,3,2,1:T(8,128)(2,1)} %bitcast.64, bf16[512,2,40]{0,2,1:T(8,128)(2,1)} %get-tuple-element.15, bf16[512,2,40]{0,2,1:T(8,128)(2,1)S(1)} %get-tuple-element.14), kind=kOutput, calls=%fused_computation.76 | convolution fusion | flops 345571840 | bytes 9486336 | tf_op jit(solution)/shard_map/sub | solution.py:101
  139.6 4.2 fusion.22
  143.9 4.6 %fusion.54 = f32[512,2560]{1,0:T(8,128)} fusion(bf16[512,640]{0,1:T(8,128)(2,1)S(1)} %bitcast.62, bf16[640,2560]{1,0:T(8,128)(2,1)S(1)} %copy-done), kind=kOutput, calls=%fused_computation.77 | convolution fusion | flops 1677721600 | bytes 9175040 | tf_op jit(solution)/shard_map/dot_general | solution.py:105
  148.6 2.4 convert_element_type.68
  151.0 1.3 all_to_all.33
  152.4 19.2 %all_to_all.41 = bf16[20,4,3456]{2,0,1:T(8,128)(2,1)} all-to-all(bf16[20,4,3456]{2,0,1:T(8,128)(2,1)S(1)} %copy.20), channel_id=1, replica_groups=mesh['req'=32,'tp'=4] {'tp'}, dimensions={1} | all-to-all | bytes 1105920 | tf_op jit(solution)/shard_map/all_to_all | solution.py:61
  171.6 2.0 all_to_all.36
  174.8 89.1 %all-reduce.2.cloned.1.call-done = f32[512,2560]{1,0:T(8,128)} async-done(((f32[512,2560]{1,0:T(8,128)}), f32[512,2560]{1,0:T(8,128)}) %all-reduce.2.cloned.1.call-update) | async-done | bytes 5242896 | tf_op jit(solution)/shard_map/psum | solution.py:110
  264.0 5.4 %multiply_reduce_fusion = (f32[512]{0:T(512)S(1)}, f32[512,2560]{1,0:T(8,128)}) fusion(f32[512,2560]{1,0:T(8,128)} %all-reduce.2.cloned.1.call-done, bf16[512,2560]{1,0:T(8,128)(2,1)S(1)} %copy-done.2), kind=kLoop, calls=%fused_computation.17 | loop fusion | flops 5242368 | bytes 13109248 | tf_op jit(solution)/shard_map/reduce_sum | solution.py:13
  269.4 25.0 %reshape.163 = bf16[128,20,3456]{2,1,0:T(8,128)(2,1)} reshape(bf16[2560,3456]{1,0:T(8,128)(2,1)} %all-gather.3.cloned.1.call-done) | data formatting | bytes 35389440 | tf_op jit(solution)/shard_map/reshape | solution.py:81
  294.3 17.7 %gather_fusion.1 = bf16[128,20,3456]{2,1,0:T(8,128)(2,1)} fusion(bf16[128,20,3456]{2,1,0:T(8,128)(2,1)} %reshape.163, s32[1024]{0:T(1024)S(1)} %pad_clamp_fusion), kind=kCustom, calls=%fused_computation.1 | custom fusion | bytes 35389952 | tf_op jit(solution)/shard_map/gather | solution.py:81
  312.0 24.8 %reshape.164 = bf16[2560,3456]{1,0:T(8,128)(2,1)} reshape(bf16[128,20,3456]{2,1,0:T(8,128)(2,1)} %gather_fusion.1) | data formatting | bytes 35389440 | tf_op jit(solution)/shard_map/reshape | solution.py:81
  336.8 15.3 %fusion.12 = f32[512,3456]{1,0:T(8,128)S(1)} fusion(bf16[2560,3456]{1,0:T(8,128)(2,1)} %reshape.164, f32[512,2560]{1,0:T(8,128)} %get-tuple-element.11, f32[2560]{0:T(1024)S(1)} %copy-done.8, f32[512]{0:T(512)S(1)} %add_rsqrt_fusion), kind=kOutput, calls=%fused_computation.24 | convolution fusion | flops 9063628800 | bytes 30027776 | tf_op jit(solution)/shard_map/dot_general | solution.py:114
  352.1 10.4 %fusion.19 = f32[512,2560]{1,0:T(8,128)} fusion(bf16[1728,2560]{1,0:T(8,128)(2,1)} %param.19, f32[512,3456]{1,0:T(8,128)S(1)} %fusion.12), kind=kOutput, calls=%fused_computation.30 | convolution fusion | flops 4535156736 | bytes 21430272 | tf_op jit(solution)/shard_map/dot_general | solution.py:116
  363.2 9.9 %fusion.23 = bf16[4,128,320]{1,0,2:T(4,128)(2,1)S(1)} fusion(bf16[128,128,320]{1,2,0:T(8,128)(2,1)} %all-gather.5.cloned.1.call-done, s32[128]{0:T(128)S(1)} %copy-done.6, s32[4]{0:T(128)S(1)} %iota_add_fusion), kind=kOutput, calls=%fused_computation.34 | convolution fusion | flops 42107392 | bytes 10813968 | tf_op jit(solution)/shard_map/np,nsc->psc/dot_general | solution.py:136
  373.8 44.2 %reduce-scatter.2.cloned.1.call-done = f32[128,2560]{1,0:T(8,128)} async-done(((f32[512,2560]{1,0:T(8,128)}), f32[128,2560]{1,0:T(8,128)}) %reduce-scatter.2.cloned.1.call-update) | async-done | bytes 1310736 | tf_op jit(solution)/shard_map/reduce_scatter | solution.py:117
  418.1 2.7 multiply_convert_fusion.2
  (54 shorter events, 5.5 us)
Async XLA Ops:
  8.0 135.9 %copy-start = (bf16[640,2560]{1,0:T(8,128)(2,1)S(1)}, bf16[640,2560]{1,0:T(8,128)(2,1)}, u32[]{:S(2)}) copy-start(bf16[640,2560]{1,0:T(8,128)(2,1)} %param.18) | copy-start | bytes 9830404
  25.7 10.9 %copy-start.9 = (s32[128]{0:T(128)S(1)}, s32[128]{0:T(128)}, u32[]{:S(2)}) copy-start(s32[128]{0:T(128)} %param.13) | copy-start | bytes 1540
  25.7 71.7 %all-to-all-start.1 = ((bf16[32,80,960]{2,1,0:T(8,128)(2,1)}), bf16[32,80,960]{2,1,0:T(8,128)(2,1)}, u32[]{:S(2)}, u32[]{:S(2)}) async-start(bf16[32,80,960]{2,1,0:T(8,128)(2,1)} %stack.5), calls=%async_computation.1 | async-start | bytes 10485760 | tf_op jit(solution)/shard_map/all_to_all | solution.py:74
  35.9 228.1 %all-reduce.2.cloned.1.call-start = ((), (), s32[]{:S(2)}) async-start(), calls=%async_computation.4 | async-start | bytes 10485760 | tf_op jit(solution)/shard_map/psum | solution.py:110
  113.5 9.8 %copy-start.7 = (f32[2560]{0:T(1024)S(1)}, f32[2560]{0:T(1024)}, u32[]{:S(2)}) copy-start(f32[2560]{0:T(1024)} %param.16) | copy-start | bytes 30724
  132.1 7.6 %copy-start.5 = (bf16[512,160]{0,1:T(8,128)(2,1)S(1)}, bf16[512,160]{0,1:T(8,128)(2,1)}, u32[]{:S(2)}) copy-start(bf16[512,160]{0,1:T(8,128)(2,1)} %get-tuple-element.9) | copy-start | bytes 491524
  148.5 25.4 %copy-start.3 = (bf16[20,4,8,128]{3,2,1,0:T(8,128)(2,1)S(1)}, bf16[20,4,8,128]{3,2,1,0:T(8,128)(2,1)}, u32[]{:S(2)}) copy-start(bf16[20,4,8,128]{3,2,1,0:T(8,128)(2,1)} %get-tuple-element.8) | copy-start | bytes 491524
  148.5 25.4 %copy-start.4 = (bf16[512,2,40]{0,2,1:T(8,128)(2,1)S(1)}, bf16[512,2,40]{0,2,1:T(8,128)(2,1)}, u32[]{:S(2)}) copy-start(bf16[512,2,40]{0,2,1:T(8,128)(2,1)} %get-tuple-element.15) | copy-start | bytes 245764
  148.5 115.5 %copy-start.2 = (bf16[512,2560]{1,0:T(8,128)(2,1)S(1)}, bf16[512,2560]{1,0:T(8,128)(2,1)}, u32[]{:S(2)}) copy-start(bf16[512,2560]{1,0:T(8,128)(2,1)} %param.10) | copy-start | bytes 7864324
  148.5 120.9 %all-gather.3.cloned.1.call-start = ((), (), s32[]{:S(2)}) async-start(), calls=%async_computation.5 | async-start | bytes 18247680 | tf_op jit(solution)/shard_map/all_gather | solution.py:76
  173.6 189.0 %all-gather.5.cloned.1.call-start = ((), (), s32[]{:S(2)}) async-start(), calls=%async_computation.7 | async-start | bytes 10813440 | tf_op jit(solution)/shard_map/all_gather | solution.py:139
  174.8 243.3 %reduce-scatter.2.cloned.1.call-start = ((), (), s32[]{:S(2)}) async-start(), calls=%async_computation.6 | async-start | bytes 6553600 | tf_op jit(solution)/shard_map/reduce_scatter | solution.py:117
  312.0 24.8 %copy-start.8 = (f32[2560]{0:T(1024)S(1)}, f32[2560]{0:T(1024)}, u32[]{:S(2)}) copy-start(f32[2560]{0:T(1024)} %param.17) | copy-start | bytes 30724
  362.5 0.7 copy-start.6
  362.6 58.2 %copy-start.1 = (bf16[640,2560]{1,0:T(8,128)(2,1)S(1)}, bf16[640,2560]{1,0:T(8,128)(2,1)}, u32[]{:S(2)}) copy-start(bf16[640,2560]{1,0:T(8,128)(2,1)} %param.18) | copy-start | bytes 9830404
Sparse Core Ops, SparseCore 0:
  148.6 115.2 all-reduce.1
  362.7 55.3 reduce-scatter.1
Sparse Core Ops, SparseCore 1:
  173.7 76.5 all-gather.2
  252.9 57.2 all-gather.4
